TPU v7x, 32 devices: a whole 2x2x4 slice. The times are simulated.
32 devices in a mesh: fsdp: 8 (over z, y), tensor: 4 (over x, core).
Axes of the slice: x: 2, y: 2, z: 4, core: 2. Of those that a mesh axis runs over, the one named last changes fastest.
Arguments:
- block_input: bfloat16 [32768, 512], P(('fsdp', 'tensor')), may hold values from -6 to 6
- segments: int32 [32768], P('fsdp'), may hold values from 0 to 6, as said below
- ln_gain: bfloat16 [512], P('fsdp'), may hold values from 0.5 to 1.5
- ln_bias: bfloat16 [512], P('fsdp'), may hold values from -3 to 3
- b_real: bfloat16 [512, 256], P('fsdp', 'tensor'), may hold values from -0.1875 to 0.1875
- b_imag: bfloat16 [512, 256], P('fsdp', 'tensor'), may hold values from -0.1875 to 0.1875
- c_real: bfloat16 [512, 256], P('fsdp', 'tensor'), may hold values from -0.25 to 0.25
- c_imag: bfloat16 [512, 256], P('fsdp', 'tensor'), may hold values from -0.25 to 0.25
- nu_log: bfloat16 [256], P('fsdp'), may hold values from -9.1875 to -3
- theta_log: bfloat16 [256], P('fsdp'), may hold values from -4 to -1
- gamma_log: bfloat16 [256], P('fsdp'), may hold values from -0.5 to 0.5
- d_skip: bfloat16 [512], P('fsdp'), may hold values from -4 to 4
- w_value: bfloat16 [512, 512], P('fsdp', 'tensor'), may hold values from -0.25 to 0.25
- w_gate: bfloat16 [512, 512], P('fsdp', 'tensor'), may hold values from -0.25 to 0.25
- b_value: bfloat16 [512], P('fsdp'), may hold values from -3 to 3
- b_gate: bfloat16 [512], P('fsdp'), may hold values from -3 to 3
- out_grad: bfloat16 [32768, 512], P(('fsdp', 'tensor')), may hold values from -6 to 6
Outputs:
- mixed: bfloat16 [32768, 512], P(('fsdp', 'tensor'))
- input_grad: float32 [32768, 512], P(('fsdp', 'tensor'))
- ln_gain_grad: float32 [512], P('fsdp')
- ln_bias_grad: float32 [512], P('fsdp')
- b_real_grad: float32 [512, 256], P('fsdp', 'tensor')
- b_imag_grad: float32 [512, 256], P('fsdp', 'tensor')
- c_real_grad: float32 [512, 256], P('fsdp', 'tensor')
- c_imag_grad: float32 [512, 256], P('fsdp', 'tensor')
- nu_grad: float32 [256], P('fsdp')
- theta_grad: float32 [256], P('fsdp')
- gamma_grad: float32 [256], P('fsdp')
- skip_grad: float32 [512], P('fsdp')
- value_weight_grad: float32 [512, 512], P('fsdp', 'tensor')
- gate_weight_grad: float32 [512, 512], P('fsdp', 'tensor')
- value_bias_grad: float32 [512], P('fsdp')
- gate_bias_grad: float32 [512], P('fsdp')
Inputs may be any that keep to these rules, and one draw needn't show every extreme that they name: `segments`: in each sequence of 2048 tokens the document numbers start at 1, rise by one at each of 5 boundaries that lie in the first three quarters, and all of 1 to 6 occur; the last 1 to 512 tokens are padding with number 0.
All inputs are finite; a program needn't handle non-finite values.
Results may differ from a plain program's by a relative error of at most 0.02.
Values may be sent and summed in bfloat16 or wider, within the bound.
No kernel may reach another device: no remote copies, remote signals or barrier semaphores. Data moves between devices by JAX's collectives and lax.ppermute only.
A program may use at most 128 MiB of HBM per device.

v0:
```python
import math
import jax
import jax.numpy as jnp
from jax import lax
from jax.sharding import PartitionSpec as P

SEQ_LEN = 2048
norm_epsilon = 1e-05


def complex_product(left, right):
    half_width = left.shape[-1] // 2
    left_re = left[..., :half_width]
    left_im = left[..., half_width:]
    right_re = right[..., :half_width]
    right_im = right[..., half_width:]
    return jnp.concatenate(
        [left_re * right_re - left_im * right_im, left_re * right_im + left_im * right_re], axis=-1
    )


def linear_chain(earlier, later):
    return (complex_product(later[0], earlier[0]), complex_product(later[0], earlier[1]) + later[1])


def blocked_chain(decay, source, reverse):
    rows, width = source.shape
    block = math.gcd(rows, 16)
    count = rows // block
    decay_blocks = decay.reshape(count, block, width)
    source_blocks = source.reshape(count, block, width)
    order = list(range(block - 1, -1, -1)) if reverse else list(range(block))
    decay_parts = [None] * block
    local_parts = [None] * block
    running_decay = None
    running_local = None
    for place in order:
        decay_here = decay_blocks[:, place]
        source_here = source_blocks[:, place]
        if running_decay is None:
            running_decay = decay_here
            running_local = source_here
        else:
            running_decay, running_local = linear_chain(
                (running_decay, running_local), (decay_here, source_here)
            )
        decay_parts[place] = running_decay
        local_parts[place] = running_local
    decay_cum = jnp.stack(decay_parts, axis=1)
    local = jnp.stack(local_parts, axis=1)
    edge = 0 if reverse else block - 1
    _, carried = lax.associative_scan(
        linear_chain, (decay_parts[edge], local_parts[edge]), reverse=reverse, axis=0
    )
    zero_row = jnp.zeros((1, width), jnp.float32)
    if reverse:
        incoming = jnp.concatenate([carried[1:], zero_row], axis=0)
    else:
        incoming = jnp.concatenate([zero_row, carried[:-1]], axis=0)
    return (local + complex_product(decay_cum, incoming[:, None, :])).reshape(rows, width)


def state_params(nu_part, theta_part, gamma_part):
    modulus = jnp.exp(-jnp.exp(nu_part))
    rotation = jnp.exp(theta_part)
    return (
        modulus * jnp.cos(rotation),
        modulus * jnp.sin(rotation),
        jnp.exp(gamma_part) * jnp.sqrt(1.0 - modulus * modulus),
    )


def contract_rows(left, right):
    return lax.dot_general(
        left, right, (((0,), (0,)), ((), ())), preferred_element_type=jnp.float32
    )


def contract_cols(left, right):
    return lax.dot_general(
        left, right, (((1,), (1,)), ((), ())), preferred_element_type=jnp.float32
    )


def shards(
    block_input,
    segments,
    ln_gain,
    ln_bias,
    b_real,
    b_imag,
    c_real,
    c_imag,
    nu_log,
    theta_log,
    gamma_log,
    d_skip,
    w_value,
    w_gate,
    b_value,
    b_gate,
    out_grad,
):
    tensor_rank = lax.axis_index("tensor")
    (
        gain_all,
        shift_all,
        nu_all,
        theta_all,
        gamma_all,
        skip_all,
        value_bias_all,
        gate_bias_all,
        breal_all,
        bimag_all,
        creal_all,
        cimag_all,
        wvalue_all,
        wgate_all,
    ) = (
        lax.all_gather(ln_gain, "fsdp", axis=0, tiled=True),
        lax.all_gather(ln_bias, "fsdp", axis=0, tiled=True),
        lax.all_gather(nu_log, "fsdp", axis=0, tiled=True),
        lax.all_gather(theta_log, "fsdp", axis=0, tiled=True),
        lax.all_gather(gamma_log, "fsdp", axis=0, tiled=True),
        lax.all_gather(d_skip, "fsdp", axis=0, tiled=True),
        lax.all_gather(b_value, "fsdp", axis=0, tiled=True),
        lax.all_gather(b_gate, "fsdp", axis=0, tiled=True),
        lax.all_gather(b_real, "fsdp", axis=0, tiled=True),
        lax.all_gather(b_imag, "fsdp", axis=0, tiled=True),
        lax.all_gather(c_real, "fsdp", axis=0, tiled=True),
        lax.all_gather(c_imag, "fsdp", axis=0, tiled=True),
        lax.all_gather(w_value, "fsdp", axis=0, tiled=True),
        lax.all_gather(w_gate, "fsdp", axis=0, tiled=True),
    )
    row_count, feature_count = block_input.shape
    group_rows = segments.shape[0]
    state_count = b_real.shape[1]
    unit_count = w_value.shape[1]
    full_states = nu_all.shape[0]
    position = jnp.arange(group_rows)
    earlier_ids = jnp.concatenate([segments[:1], segments[:-1]])
    keep = jnp.where((position % SEQ_LEN > 0) & (segments == earlier_ids), 1.0, 0.0).astype(
        jnp.float32
    )[:, None]
    keep_next = jnp.concatenate([keep[1:], jnp.zeros((1, 1), jnp.float32)], axis=0)
    live = jnp.where(segments > 0, 1.0, 0.0).astype(jnp.float32)[:, None]
    row_live = lax.dynamic_slice_in_dim(live, tensor_rank * row_count, row_count, 0)
    gain = gain_all.astype(jnp.float32)
    shift = shift_all.astype(jnp.float32)
    skip = skip_all.astype(jnp.float32)
    inputs_wide = block_input.astype(jnp.float32)
    centred = inputs_wide - jnp.mean(inputs_wide, axis=1, keepdims=True)
    inverse_std = lax.rsqrt(jnp.mean(centred * centred, axis=1, keepdims=True) + norm_epsilon)
    standard = centred * inverse_std
    normed = (standard * gain + shift).astype(jnp.bfloat16)
    normed_group = lax.all_gather(normed, "tensor", axis=0, tiled=True)
    state_start = tensor_rank * state_count
    (decay_re, decay_im, gamma), params_back = jax.vjp(
        state_params,
        lax.dynamic_slice_in_dim(nu_all.astype(jnp.float32), state_start, state_count),
        lax.dynamic_slice_in_dim(theta_all.astype(jnp.float32), state_start, state_count),
        lax.dynamic_slice_in_dim(gamma_all.astype(jnp.float32), state_start, state_count),
    )
    rate_pair = jnp.concatenate([decay_re, decay_im])
    gamma_pair = jnp.concatenate([gamma, gamma])
    conj_sign = jnp.concatenate(
        [jnp.ones((state_count,), jnp.float32), -jnp.ones((state_count,), jnp.float32)]
    )
    input_pack = jnp.concatenate([breal_all, bimag_all], axis=1)
    output_pack = jnp.concatenate([creal_all, -cimag_all], axis=1)
    drive = jnp.dot(normed_group, input_pack, preferred_element_type=jnp.float32)
    decay = keep * rate_pair
    hidden = blocked_chain(decay, gamma_pair * live * drive, False)
    hidden_low = hidden.astype(jnp.bfloat16)
    state_total = lax.psum_scatter(
        contract_cols(hidden_low, output_pack), "tensor", scatter_dimension=0, tiled=True
    )
    normed_wide = normed.astype(jnp.float32)
    lru_out = state_total + skip * normed_wide
    activated, gelu_back = jax.vjp(jax.nn.gelu, lru_out)
    act = activated.astype(jnp.bfloat16)
    unit_start = tensor_rank * unit_count
    act_group = lax.all_gather(act, "tensor", axis=0, tiled=True)
    value_shift = lax.dynamic_slice_in_dim(
        value_bias_all.astype(jnp.float32), unit_start, unit_count
    )
    gate_shift = lax.dynamic_slice_in_dim(gate_bias_all.astype(jnp.float32), unit_start, unit_count)
    value = jnp.dot(act_group, wvalue_all, preferred_element_type=jnp.float32) + value_shift
    gate = jnp.dot(act_group, wgate_all, preferred_element_type=jnp.float32) + gate_shift
    opening = jax.nn.sigmoid(gate)
    gated_units = (value * opening).astype(jnp.bfloat16)
    gated_mine = lax.all_to_all(gated_units, "tensor", split_axis=0, concat_axis=1, tiled=True)
    mixed = (inputs_wide + row_live * gated_mine.astype(jnp.float32)).astype(jnp.bfloat16)
    cotangent = out_grad.astype(jnp.float32)
    gated_grad = (row_live * cotangent).astype(jnp.bfloat16)
    gated_grad_units = lax.all_to_all(
        gated_grad, "tensor", split_axis=1, concat_axis=0, tiled=True
    ).astype(jnp.float32)
    value_grad = (gated_grad_units * opening).astype(jnp.bfloat16)
    gate_grad = (gated_grad_units * value * opening * (1.0 - opening)).astype(jnp.bfloat16)
    value_weight_grad = contract_rows(act_group, value_grad)
    gate_weight_grad = contract_rows(act_group, gate_grad)
    value_bias_grad = lax.dynamic_update_slice(
        jnp.zeros((feature_count,), jnp.float32),
        jnp.sum(value_grad.astype(jnp.float32), axis=0),
        (unit_start,),
    )
    gate_bias_grad = lax.dynamic_update_slice(
        jnp.zeros((feature_count,), jnp.float32),
        jnp.sum(gate_grad.astype(jnp.float32), axis=0),
        (unit_start,),
    )
    act_grad = lax.psum_scatter(
        contract_cols(value_grad, wvalue_all) + contract_cols(gate_grad, wgate_all),
        "tensor",
        scatter_dimension=0,
        tiled=True,
    )
    lru_grad = gelu_back(act_grad)[0].astype(jnp.bfloat16)
    lru_grad_wide = lru_grad.astype(jnp.float32)
    skip_grad = jnp.sum(lru_grad_wide * normed_wide, axis=0)
    lru_grad_group = lax.all_gather(lru_grad, "tensor", axis=0, tiled=True)
    state_grad = jnp.dot(lru_grad_group, output_pack, preferred_element_type=jnp.float32)
    output_pack_grad = contract_rows(lru_grad_group, hidden_low)
    next_decay = keep_next * (rate_pair * conj_sign)
    total_grad = blocked_chain(next_decay, state_grad, True)
    rate_grad = jnp.sum(keep[1:] * complex_product(hidden[:-1] * conj_sign, total_grad[1:]), axis=0)
    gamma_terms = jnp.sum(live * drive * total_grad, axis=0)
    nu_part_grad, theta_part_grad, gamma_part_grad = params_back(
        (
            rate_grad[:state_count],
            rate_grad[state_count:],
            gamma_terms[:state_count] + gamma_terms[state_count:],
        )
    )
    empty_states = jnp.zeros((full_states,), jnp.float32)
    nu_grad = lax.dynamic_update_slice(empty_states, nu_part_grad, (state_start,))
    theta_grad = lax.dynamic_update_slice(empty_states, theta_part_grad, (state_start,))
    gamma_grad = lax.dynamic_update_slice(empty_states, gamma_part_grad, (state_start,))
    drive_grad = (gamma_pair * live * total_grad).astype(jnp.bfloat16)
    input_pack_grad = contract_rows(normed_group, drive_grad)
    state_part = lax.psum_scatter(
        contract_cols(drive_grad, input_pack).astype(jnp.bfloat16),
        "tensor",
        scatter_dimension=0,
        tiled=True,
    ).astype(jnp.float32)
    normed_grad = state_part + lru_grad_wide * skip
    standard_grad = normed_grad * gain
    gain_grad = jnp.sum(normed_grad * standard, axis=0)
    shift_grad = jnp.sum(normed_grad, axis=0)
    input_grad = cotangent + inverse_std * (
        standard_grad
        - jnp.mean(standard_grad, axis=1, keepdims=True)
        - standard * jnp.mean(standard_grad * standard, axis=1, keepdims=True)
    )
    summed = (
        lax.psum_scatter(gain_grad, "fsdp", scatter_dimension=0, tiled=True),
        lax.psum_scatter(shift_grad, "fsdp", scatter_dimension=0, tiled=True),
        lax.psum_scatter(nu_grad, "fsdp", scatter_dimension=0, tiled=True),
        lax.psum_scatter(theta_grad, "fsdp", scatter_dimension=0, tiled=True),
        lax.psum_scatter(gamma_grad, "fsdp", scatter_dimension=0, tiled=True),
        lax.psum_scatter(skip_grad, "fsdp", scatter_dimension=0, tiled=True),
        lax.psum_scatter(value_bias_grad, "fsdp", scatter_dimension=0, tiled=True),
        lax.psum_scatter(gate_bias_grad, "fsdp", scatter_dimension=0, tiled=True),
        lax.psum_scatter(input_pack_grad[:, :state_count], "fsdp", scatter_dimension=0, tiled=True),
        lax.psum_scatter(input_pack_grad[:, state_count:], "fsdp", scatter_dimension=0, tiled=True),
        lax.psum_scatter(
            output_pack_grad[:, :state_count], "fsdp", scatter_dimension=0, tiled=True
        ),
        lax.psum_scatter(
            -output_pack_grad[:, state_count:], "fsdp", scatter_dimension=0, tiled=True
        ),
        lax.psum_scatter(value_weight_grad, "fsdp", scatter_dimension=0, tiled=True),
        lax.psum_scatter(gate_weight_grad, "fsdp", scatter_dimension=0, tiled=True),
    )
    vectors = lax.psum(
        (summed[0], summed[1], summed[2], summed[3], summed[4], summed[5], summed[6], summed[7]),
        "tensor",
    )
    return (
        mixed,
        input_grad,
        vectors[0],
        vectors[1],
        summed[8],
        summed[9],
        summed[10],
        summed[11],
        vectors[2],
        vectors[3],
        vectors[4],
        vectors[5],
        summed[12],
        summed[13],
        vectors[6],
        vectors[7],
    )


def solution(mesh):
    in_specs = (
        P(("fsdp", "tensor"), None),
        P("fsdp"),
        P("fsdp"),
        P("fsdp"),
        P("fsdp", "tensor"),
        P("fsdp", "tensor"),
        P("fsdp", "tensor"),
        P("fsdp", "tensor"),
        P("fsdp"),
        P("fsdp"),
        P("fsdp"),
        P("fsdp"),
        P("fsdp", "tensor"),
        P("fsdp", "tensor"),
        P("fsdp"),
        P("fsdp"),
        P(("fsdp", "tensor"), None),
    )
    out_specs = (
        P(("fsdp", "tensor"), None),
        P(("fsdp", "tensor"), None),
        P("fsdp"),
        P("fsdp"),
        P("fsdp", "tensor"),
        P("fsdp", "tensor"),
        P("fsdp", "tensor"),
        P("fsdp", "tensor"),
        P("fsdp"),
        P("fsdp"),
        P("fsdp"),
        P("fsdp"),
        P("fsdp", "tensor"),
        P("fsdp", "tensor"),
        P("fsdp"),
        P("fsdp"),
    )
    return jax.shard_map(shards, mesh=mesh, in_specs=in_specs, out_specs=out_specs, check_vma=False)
```

profile of v0, /device:TPU:0, one launch (start us, length us, event | category | flops | bytes accessed | tf_op | source)
XLA Modules:
  0.0 1045.8 jit_solution(13006507848595677849)
XLA Ops:
  16.7 23.9 %all-reduce.52 = (bf16[512]{0:T(512)(128)(2,1)}, bf16[512]{0:T(512)(128)(2,1)}, bf16[256]{0:T(256)(128)(2,1)S(1)}, bf16[256]{0:T(256)(128)(2,1)S(1)}, bf16[512]{...) all-reduce(bf16[512]{0:T(512)(128)(2,1)S(1)} %dynamic-update-slice., ...), channel_id=1, replica_groups=mesh['fsdp'=8,'tensor'=4] {'fsdp'}, use_global_device_ids=true, to_apply=%add.40 | all-reduce | flops 3328 | bytes 13312
  42.1 1.7 fusion.16
  48.2 30.5 %all_gather.60 = bf16[512,64]{1,0:T(8,128)(2,1)S(1)} all-gather(bf16[64,64]{1,0:T(8,128)(2,1)S(1)} %copy-done.229), channel_id=1, replica_groups=mesh['fsdp'=8,'tensor'=4] {'fsdp'}, dimensions={0}, use_global_device_ids=true | all-gather | bytes 73728 | tf_op jit(solution)/shard_map/all_gather | solution.py:132
  78.8 32.5 %all_gather.56 = bf16[512,64]{1,0:T(8,128)(2,1)} all-gather(bf16[64,64]{1,0:T(8,128)(2,1)S(1)} %copy-done.230), channel_id=1, replica_groups=mesh['fsdp'=8,'tensor'=4] {'fsdp'}, dimensions={0}, use_global_device_ids=true | all-gather | bytes 73728 | tf_op jit(solution)/shard_map/all_gather | solution.py:129
  111.3 32.5 %all_gather.57 = bf16[512,64]{1,0:T(8,128)(2,1)} all-gather(bf16[64,64]{1,0:T(8,128)(2,1)S(1)} %copy-done.231), channel_id=1, replica_groups=mesh['fsdp'=8,'tensor'=4] {'fsdp'}, dimensions={0}, use_global_device_ids=true | all-gather | bytes 73728 | tf_op jit(solution)/shard_map/all_gather | solution.py:130
  143.8 30.5 %all_gather.59 = bf16[512,64]{1,0:T(8,128)(2,1)S(1)} all-gather(bf16[64,64]{1,0:T(8,128)(2,1)S(1)} %copy-done.232), channel_id=1, replica_groups=mesh['fsdp'=8,'tensor'=4] {'fsdp'}, dimensions={0}, use_global_device_ids=true | all-gather | bytes 73728 | tf_op jit(solution)/shard_map/all_gather | solution.py:131
  175.2 2.3 broadcast_multiply_fusion
  190.3 5.0 multiply_multiply_fusion.3
  195.3 2.5 fusion.98
  214.0 2.6 copy.194
  216.5 6.0 stack.153
  222.6 1.7 multiply_subtract_fusion.2
  225.0 4.6 fusion.39
  230.3 68.5 %reduce-scatter.18.cloned.1.call-done = f32[1024,512]{1,0:T(8,128)} async-done(((f32[4096,512]{1,0:T(8,128)}), f32[1024,512]{1,0:T(8,128)}) %reduce-scatter.18.cloned.1.call-update) | async-done | bytes 2097168 | tf_op jit(solution)/shard_map/reduce_scatter | solution.py:176
  298.8 3.5 multiply_convert_fusion.1
  302.4 2.6 copy_bitcast_fusion
  304.9 4.2 all-to-all-start.1
  309.4 30.6 %all_gather.63 = bf16[512,128]{1,0:T(8,128)(2,1)S(1)} all-gather(bf16[64,128]{1,0:T(8,128)(2,1)S(1)} %copy-done.233), channel_id=1, replica_groups=mesh['fsdp'=8,'tensor'=4] {'fsdp'}, dimensions={0}, use_global_device_ids=true | all-gather | bytes 147456 | tf_op jit(solution)/shard_map/all_gather | solution.py:133
  340.1 30.5 %all_gather.65 = bf16[512,128]{1,0:T(8,128)(2,1)S(1)} all-gather(bf16[64,128]{1,0:T(8,128)(2,1)S(1)} %copy-done.234), channel_id=1, replica_groups=mesh['fsdp'=8,'tensor'=4] {'fsdp'}, dimensions={0}, use_global_device_ids=true | all-gather | bytes 147456 | tf_op jit(solution)/shard_map/all_gather | solution.py:134
  370.6 4.8 convolution_add_fusion.2
  375.4 6.0 convert_reduce_fusion.1
  382.8 4.6 convolution_add_fusion
  387.4 73.1 %reduce-scatter.20.cloned.1.call-done = f32[1024,512]{1,0:T(8,128)} async-done(((f32[4096,512]{1,0:T(8,128)}), f32[1024,512]{1,0:T(8,128)}) %reduce-scatter.20.cloned.1.call-update) | async-done | bytes 2097168 | tf_op jit(solution)/shard_map/reduce_scatter | solution.py:214
  460.5 4.5 fusion.28
  465.4 2.5 fusion.97
  480.0 19.6 %all-gather.8.cloned.1.call-done = bf16[4096,512]{1,0:T(8,128)(2,1)} async-done(((bf16[1024,512]{1,0:T(8,128)(2,1)}), bf16[4096,512]{1,0:T(8,128)(2,1)}) %all-gather.8.cloned.1.call-update) | async-done | bytes 4194320 | tf_op jit(solution)/shard_map/all_gather | solution.py:223
  499.6 3.6 fusion.71
  503.2 2.4 fusion.96
  515.9 1.5 slice.2051
  517.4 1.5 slice.1933
  519.9 1.5 fusion.102
  523.5 1.6 fusion.100
  525.1 1.5 slice.1940
  526.6 1.5 slice.1938
  531.0 1.6 multiply_subtract_fusion.64
  534.1 1.5 slice.1934
  538.4 1.6 multiply_subtract_fusion.70
  552.2 1.5 slice.1922
  570.0 1.6 slice_add_fusion.17
  571.6 1.7 slice.2054
  580.6 2.5 copy.229
  583.1 7.8 stack.171
  591.0 3.0 multiply_subtract_fusion.1
  594.4 1.9 multiply_reduce_fusion
  597.7 3.0 convolution_convert_fusion
  602.1 4.5 fusion.108
  606.6 1.5 slice_multiply_fusion
  608.1 4.4 all-to-all-start
  613.6 4.5 fusion.109
  618.2 3.7 fusion.37
  622.8 6.8 multiply_subtract_fusion
  630.7 3.8 fusion.90
  636.5 2.9 fusion.30
  640.8 10.1 reduce-scatter.22.cloned.1.call-done
  650.8 2.9 fusion.15
  653.7 37.2 %all-reduce.50 = (f32[512]{0:T(512)S(1)}, f32[512]{0:T(512)S(1)}, f32[256]{0:T(256)S(1)}, f32[256]{0:T(256)S(1)}, f32[256]{0:T(256)S(1)}, /*index=5*/f32[512]{0:T(512)S(1)}, f32[512]{0:T(512)S(1)}, f32[512]{0:T(512)S(1)}) all-reduce(f32[512]{0:T(512)S(1)} %get-tuple-element.64, ...), channel_id=5, replica_groups=mesh['fsdp'=8,'tensor'=4] {'fsdp'}, use_global_device_ids=true, to_apply=%region_8.9.clone | all-reduce | flops 3328 | bytes 26624
  691.5 6.3 all-reduce.51
  697.8 3.8 convert_add_fusion.1
  701.6 14.8 %reduce-scatter.24.cloned.1.call-done = f32[64,128]{1,0:T(8,128)} async-done(((f32[512,128]{1,0:T(8,128)}), f32[64,128]{1,0:T(8,128)}) %reduce-scatter.24.cloned.1.call-update) | async-done | bytes 32784 | tf_op jit(solution)/shard_map/reduce_scatter | solution.py:275
  716.3 64.5 %reduce-scatter.26.cloned.1.call-done = f32[64,128]{1,0:T(8,128)} async-done(((f32[512,128]{1,0:T(8,128)}), f32[64,128]{1,0:T(8,128)}) %reduce-scatter.26.cloned.1.call-update) | async-done | bytes 32784 | tf_op jit(solution)/shard_map/reduce_scatter | solution.py:276
  780.8 64.5 %reduce-scatter.34.cloned.1.call-done = f32[64,64]{1,0:T(8,128)} async-done(((f32[512,64]{1,0:T(8,128)}), f32[64,64]{1,0:T(8,128)}) %reduce-scatter.34.cloned.1.call-update) | async-done | bytes 16400
  845.3 64.4 %reduce-scatter.32.cloned.1.call-done = f32[64,64]{1,0:T(8,128)} async-done(((f32[512,64]{1,0:T(8,128)}), f32[64,64]{1,0:T(8,128)}) %reduce-scatter.32.cloned.1.call-update) | async-done | bytes 16400
  909.7 64.5 %reduce-scatter.30.cloned.1.call-done = f32[64,64]{1,0:T(8,128)} async-done(((f32[512,64]{1,0:T(8,128)}), f32[64,64]{1,0:T(8,128)}) %reduce-scatter.30.cloned.1.call-update) | async-done | bytes 16400
  974.3 64.4 %reduce-scatter.28.cloned.1.call-done = f32[64,64]{1,0:T(8,128)} async-done(((f32[512,64]{1,0:T(8,128)}), f32[64,64]{1,0:T(8,128)}) %reduce-scatter.28.cloned.1.call-update) | async-done | bytes 16400
  (969 shorter events, 120.8 us)
Async XLA Ops:
  7.2 37.3 %copy-start = (bf16[1024,512]{1,0:T(8,128)(2,1)S(1)}, bf16[1024,512]{1,0:T(8,128)(2,1)}, u32[]{:S(2)}) copy-start(bf16[1024,512]{1,0:T(8,128)(2,1)} %param.17) | copy-start | bytes 3145732
  7.2 183.1 %all-gather.4.cloned.1.call-start = ((), (), s32[]{:S(2)}) async-start(), calls=%async_computation.11 | async-start | bytes 5242880 | tf_op jit(solution)/shard_map/all_gather | solution.py:157
  44.4 34.3 %copy-start.230 = (bf16[64,64]{1,0:T(8,128)(2,1)S(1)}, bf16[64,64]{1,0:T(8,128)(2,1)}, u32[]{:S(2)}) copy-start(bf16[64,64]{1,0:T(8,128)(2,1)} %param.21) | copy-start | bytes 24580
  44.4 66.8 %copy-start.231 = (bf16[64,64]{1,0:T(8,128)(2,1)S(1)}, bf16[64,64]{1,0:T(8,128)(2,1)}, u32[]{:S(2)}) copy-start(bf16[64,64]{1,0:T(8,128)(2,1)} %param.22) | copy-start | bytes 24580
  44.4 99.4 %copy-start.232 = (bf16[64,64]{1,0:T(8,128)(2,1)S(1)}, bf16[64,64]{1,0:T(8,128)(2,1)}, u32[]{:S(2)}) copy-start(bf16[64,64]{1,0:T(8,128)(2,1)} %param.23) | copy-start | bytes 24580
  44.4 130.7 %copy-start.249 = (f32[128]{0:T(128)S(1)}, f32[128]{0:T(128)}, u32[]{:S(2)}) copy-start(f32[128]{0:T(128)} %constant.70.clone.1) | copy-start | bytes 1540
  45.9 252.9 %reduce-scatter.18.cloned.1.call-start = ((), (), s32[]{:S(2)}) async-start(), calls=%async_computation.12 | async-start | bytes 10485760 | tf_op jit(solution)/shard_map/reduce_scatter | solution.py:176
  47.4 130.2 %copy-start.245 = (f32[256]{0:T(256)}, f32[256]{0:T(256)S(1)}, u32[]{:S(2)}) copy-start(f32[256]{0:T(256)S(1)} %convert_element_type.102) | copy-start | bytes 3076
  47.4 130.1 %copy-start.247 = (f32[256]{0:T(256)}, f32[256]{0:T(256)S(1)}, u32[]{:S(2)}) copy-start(f32[256]{0:T(256)S(1)} %convert_element_type.97) | copy-start | bytes 3076
  47.4 130.1 %copy-start.251 = (f32[256]{0:T(256)}, f32[256]{0:T(256)S(1)}, u32[]{:S(2)}) copy-start(f32[256]{0:T(256)S(1)} %convert_element_type.98) | copy-start | bytes 3076
  78.8 146.2 %copy-start.36 = (bf16[512,64]{1,0:T(8,128)(2,1)}, bf16[512,64]{1,0:T(8,128)(2,1)S(1)}, u32[]{:S(2)}) copy-start(bf16[512,64]{1,0:T(8,128)(2,1)S(1)} %neg.22) | copy-start | bytes 196612
  174.3 50.6 %copy-start.37 = (bf16[512,64]{1,0:T(8,128)(2,1)}, bf16[512,64]{1,0:T(8,128)(2,1)S(1)}, u32[]{:S(2)}) copy-start(bf16[512,64]{1,0:T(8,128)(2,1)S(1)} %all_gather.59) | copy-start | bytes 196612
  179.8 9.8 copy-start.38
  207.0 5.8 copy-start.89
  207.0 5.8 copy-start.165
  207.0 5.8 copy-start.167
  229.6 69.2 %copy-start.212 = (f32[1024]{0:T(1024)S(1)}, f32[1024]{0:T(1024)}, u32[]{:S(2)}) copy-start(f32[1024]{0:T(1024)} %copy-done.211) | copy-start | bytes 12292
  229.6 69.2 %copy-start.215 = (f32[1024]{0:T(1024)S(1)}, f32[1024]{0:T(1024)}, u32[]{:S(2)}) copy-start(f32[1024]{0:T(1024)} %copy-done.214) | copy-start | bytes 12292
  229.6 69.2 %copy-start.219 = (f32[512]{0:T(512)S(1)}, f32[512]{0:T(512)}, u32[]{:S(2)}) copy-start(f32[512]{0:T(512)} %copy-done.218) | copy-start | bytes 6148
  229.6 69.2 %copy-start.225 = (f32[512]{0:T(512)S(1)}, f32[512]{0:T(512)}, u32[]{:S(2)}) copy-start(f32[512]{0:T(512)} %copy-done.224) | copy-start | bytes 6148
  229.6 140.9 %all-gather.6.cloned.1.call-start = ((), (), s32[]{:S(2)}) async-start(), calls=%async_computation.13 | async-start | bytes 5242880 | tf_op jit(solution)/shard_map/all_gather | solution.py:184
  230.3 230.2 %copy-start.222 = (f32[512]{0:T(512)}, f32[512]{0:T(512)S(1)}, u32[]{:S(2)}) copy-start(f32[512]{0:T(512)S(1)} %convert_element_type.104) | copy-start | bytes 6148
  302.3 6.9 copy-start.255
  302.3 7.0 copy-start.254
  302.4 7.1 copy-start.233
  302.4 37.7 %copy-start.234 = (bf16[64,128]{1,0:T(8,128)(2,1)S(1)}, bf16[64,128]{1,0:T(8,128)(2,1)}, u32[]{:S(2)}) copy-start(bf16[64,128]{1,0:T(8,128)(2,1)} %param.30) | copy-start | bytes 49156
  304.9 70.4 %all-to-all-start.1 = ((bf16[1024,4,128]{2,0,1:T(8,128)(2,1)}), bf16[1024,4,128]{2,0,1:T(8,128)(2,1)}, u32[]{:S(2)}, u32[]{:S(2)}) async-start(bf16[1024,4,128]{2,0,1:T(8,128)(2,1)} %copy_bitcast_fusion), calls=%async_computation.2 | async-start | bytes 2097152 | tf_op jit(solution)/shard_map/all_to_all | solution.py:197
  309.2 151.3 %reduce-scatter.20.cloned.1.call-start = ((), (), s32[]{:S(2)}) async-start(), calls=%async_computation.14 | async-start | bytes 10485760 | tf_op jit(solution)/shard_map/reduce_scatter | solution.py:214
  387.4 112.3 %all-gather.8.cloned.1.call-start = ((), (), s32[]{:S(2)}) async-start(), calls=%async_computation.15 | async-start | bytes 5242880 | tf_op jit(solution)/shard_map/all_gather | solution.py:223
  465.0 185.8 %reduce-scatter.22.cloned.1.call-start = ((), (), s32[]{:S(2)}) async-start(), calls=%async_computation.16 | async-start | bytes 5242880 | tf_op jit(solution)/shard_map/reduce_scatter | solution.py:243
  469.5 9.8 copy-start.40
  469.5 9.8 copy-start.42
  511.6 21.8 %copy-start.102 = (f32[256,64]{1,0:T(8,128)}, f32[256,64]{1,0:T(8,128)S(1)}, u32[]{:S(2)}) copy-start(f32[256,64]{1,0:T(8,128)S(1)} %get-tuple-element.248) | copy-start | bytes 196612
  523.5 28.1 %copy-start.205 = (f32[127,128]{1,0:T(8,128)S(1)}, f32[127,128]{1,0:T(8,128)}, u32[]{:S(2)}) copy-start(f32[127,128]{1,0:T(8,128)} %slice.1920) | copy-start | bytes 195076
  534.0 20.2 %copy-start.210 = (f32[127,128]{1,0:T(8,128)S(1)}, f32[127,128]{1,0:T(8,128)}, u32[]{:S(2)}) copy-start(f32[127,128]{1,0:T(8,128)} %slice.2051) | copy-start | bytes 195076
  570.0 9.2 copy-start.65
  571.6 7.7 copy-start.63
  573.3 5.7 copy-start.67
  573.3 5.7 copy-start.155
  573.3 5.7 copy-start.157
  573.3 5.8 copy-start.140
  573.3 5.8 copy-start.142
  573.3 6.0 copy-start.136
  573.3 6.0 copy-start.138
  583.1 7.8 copy-start.208
  583.1 7.8 copy-start.209
  600.7 115.6 %reduce-scatter.24.cloned.1.call-start = ((), (), s32[]{:S(2)}) async-start(), calls=%async_computation.17 | async-start | bytes 294912 | tf_op jit(solution)/shard_map/reduce_scatter | solution.py:275
  608.1 89.7 %all-to-all-start = ((bf16[4,1024,128]{2,1,0:T(8,128)(2,1)}), bf16[4,1024,128]{2,1,0:T(8,128)(2,1)}, u32[]{:S(2)}, u32[]{:S(2)}) async-start(bf16[4,1024,128]{2,1,0:T(8,128)(2,1)} %bitcast.520), calls=%async_computation.1 | async-start | bytes 2097152 | tf_op jit(solution)/shard_map/all_to_all | solution.py:193
  612.5 168.3 %reduce-scatter.26.cloned.1.call-start = ((), (), s32[]{:S(2)}) async-start(), calls=%async_computation.18 | async-start | bytes 294912 | tf_op jit(solution)/shard_map/reduce_scatter | solution.py:276
  618.1 227.2 %reduce-scatter.34.cloned.1.call-start = ((), (), s32[]{:S(2)}) async-start(), calls=%async_computation.22 | async-start | bytes 294912
  622.8 8.0 copy-start.2
  622.8 287.0 %reduce-scatter.32.cloned.1.call-start = ((), (), s32[]{:S(2)}) async-start(), calls=%async_computation.21 | async-start | bytes 294912
  630.5 343.8 %reduce-scatter.30.cloned.1.call-start = ((), (), s32[]{:S(2)}) async-start(), calls=%async_computation.20 | async-start | bytes 294912
  636.3 402.4 %reduce-scatter.28.cloned.1.call-start = ((), (), s32[]{:S(2)}) async-start(), calls=%async_computation.19 | async-start | bytes 294912
  636.4 14.4 %copy-start.3 = (bf16[1024,512]{1,0:T(8,128)(2,1)S(1)}, bf16[1024,512]{1,0:T(8,128)(2,1)}, u32[]{:S(2)}) copy-start(bf16[1024,512]{1,0:T(8,128)(2,1)} %fusion.28) | copy-start | bytes 3145732
  636.4 14.4 %copy-start.213 = (f32[1024]{0:T(1024)S(1)}, f32[1024]{0:T(1024)}, u32[]{:S(2)}) copy-start(f32[1024]{0:T(1024)} %copy-done.211) | copy-start | bytes 12292
  636.4 14.4 %copy-start.216 = (f32[1024]{0:T(1024)S(1)}, f32[1024]{0:T(1024)}, u32[]{:S(2)}) copy-start(f32[1024]{0:T(1024)} %copy-done.214) | copy-start | bytes 12292
  636.4 14.4 %copy-start.220 = (f32[512]{0:T(512)S(1)}, f32[512]{0:T(512)}, u32[]{:S(2)}) copy-start(f32[512]{0:T(512)} %copy-done.218) | copy-start | bytes 6148
  636.5 14.4 %copy-start.223 = (f32[512]{0:T(512)S(1)}, f32[512]{0:T(512)}, u32[]{:S(2)}) copy-start(f32[512]{0:T(512)} %copy-done.222) | copy-start | bytes 6148
  636.5 14.4 %copy-start.226 = (f32[512]{0:T(512)S(1)}, f32[512]{0:T(512)}, u32[]{:S(2)}) copy-start(f32[512]{0:T(512)} %copy-done.224) | copy-start | bytes 6148
  639.4 14.4 %copy-start.241 = (f32[512]{0:T(512)S(1)}, f32[512]{0:T(512)}, u32[]{:S(2)}) copy-start(f32[512]{0:T(512)} %copy-done.240) | copy-start | bytes 6148
  639.4 14.4 %copy-start.243 = (f32[512]{0:T(512)S(1)}, f32[512]{0:T(512)}, u32[]{:S(2)}) copy-start(f32[512]{0:T(512)} %copy-done.242) | copy-start | bytes 6148
  639.4 58.4 %copy-start.8 = (bf16[1024,512]{1,0:T(8,128)(2,1)S(1)}, bf16[1024,512]{1,0:T(8,128)(2,1)}, u32[]{:S(2)}) copy-start(bf16[1024,512]{1,0:T(8,128)(2,1)} %param.33) | copy-start | bytes 3145732
  639.4 58.4 %copy-start.228 = (f32[1024]{0:T(1024)S(1)}, f32[1024]{0:T(1024)}, u32[]{:S(2)}) copy-start(f32[1024]{0:T(1024)} %copy-done.227) | copy-start | bytes 12292
  (208 other events, 460.3 us)
Sparse Core Ops, SparseCore 0:
  46.0 31.7 all-gather.3
  229.8 68.9 reduce-scatter.17
  302.4 45.2 all-gather.5
  387.5 72.9 reduce-scatter.19
  465.1 34.4 all-gather.7
  600.8 49.9 reduce-scatter.21
  655.1 61.2 reduce-scatter.23
  720.6 60.1 reduce-scatter.25
  785.1 60.2 reduce-scatter.33
  849.5 60.2 reduce-scatter.31
  914.0 60.2 reduce-scatter.29
  978.4 60.2 reduce-scatter.27
where the time goes:
time: 1050 us
  waiting for transfers between devices  509 us (48%)
  blocking collectives  255 us (24%)
  other arithmetic  114 us (11%)
  local copies, waits for them, and re-layouts  88 us (8%)
  matrix products  49.3 us (5%)
  between operations  21.5 us (2%)
    unnamed x16, waiting for transfers between devices  258 us
    reduce_scatter x1, waiting for transfers between devices, shards(): lax.psum_scatter(contract_cols(value_grad, wvalue_all) + contract_cols(ga...  73.1 us
    reduce_scatter x1, waiting for transfers between devices, shards(): lax.psum_scatter(contract_cols(hidden_low, output_pack), 'tensor', scatte...  68.5 us
    reduce_scatter x1, waiting for transfers between devices, shards(): lax.psum_scatter(gate_weight_grad, 'fsdp', scatter_dimension=0, tiled=True)  64.5 us
    unnamed x2, blocking collectives  61.1 us
    all_gather x1, blocking collectives, shards(): lax.all_gather(b_imag, 'fsdp', axis=0, tiled=True)  32.5 us
    all_gather x1, blocking collectives, shards(): lax.all_gather(b_real, 'fsdp', axis=0, tiled=True)  32.5 us
    all_gather x1, blocking collectives, shards(): lax.all_gather(w_value, 'fsdp', axis=0, tiled=True)  30.6 us
  transfers between devices with their start and end apart: 14, of which 10 were waited for; matrix products, arithmetic and copies ran while one was open for 8% of the time, Pallas kernels for 0%

commit v1 on v0

--- a/solution.py
+++ b/solution.py
@@ -6,6 +6,12 @@
 
 SEQ_LEN = 2048
 norm_epsilon = 1e-05
+
+
+def create_the_outputs(tile_in):
+    return jnp.concatenate(
+        lax.all_to_all(jnp.stack(lax.psum(1, "fsdp") * [tile_in], axis=0), "fsdp", 0, 0), 0
+    )
 
 
 def complex_product(left, right):
@@ -126,7 +132,7 @@
         lax.all_gather(d_skip, "fsdp", axis=0, tiled=True),
         lax.all_gather(b_value, "fsdp", axis=0, tiled=True),
         lax.all_gather(b_gate, "fsdp", axis=0, tiled=True),
-        lax.all_gather(b_real, "fsdp", axis=0, tiled=True),
+        create_the_outputs(b_real),
         lax.all_gather(b_imag, "fsdp", axis=0, tiled=True),
         lax.all_gather(c_real, "fsdp", axis=0, tiled=True),
         lax.all_gather(c_imag, "fsdp", axis=0, tiled=True),

time: 1050 us -> 1030 us (0.981)
  blocking collectives: 255 us -> 222 us
    all_gather x1 -> x0, blocking collectives: 32.5 us -> none  [shards(): lax.all_gather(b_real, 'fsdp', axis=0, tiled=True)]
    unnamed x548 -> x552, local copies, waits for them, and re-layouts: 20.3 us -> 22 us
  transfers between devices with their start and end apart: 14 -> 15, of which waited for: 10 -> 10; matrix products, arithmetic and copies ran while one was open for 8% -> 8% of each run, Pallas kernels for 0% -> 0%
where the time goes in v1:
time: 1030 us; the launch traced here: 1020 us
  waiting for transfers between devices  512 us (50%)
  blocking collectives  222 us (22%)
  other arithmetic  114 us (11%)
  local copies, waits for them, and re-layouts  89.7 us (9%)
  matrix products  49.3 us (5%)
  between operations  21.6 us (2%)
  starting transfers between devices  13.8 us (1%)
    unnamed x16, waiting for transfers between devices  258 us
    reduce_scatter x1, waiting for transfers between devices, shards(): lax.psum_scatter(contract_cols(value_grad, wvalue_all) + contract_cols(ga...  73 us
    reduce_scatter x1, waiting for transfers between devices, shards(): lax.psum_scatter(contract_cols(hidden_low, output_pack), 'tensor', scatte...  72.1 us
    reduce_scatter x1, waiting for transfers between devices, shards(): lax.psum_scatter(gate_weight_grad, 'fsdp', scatter_dimension=0, tiled=True)  64.6 us
    unnamed x2, blocking collectives  61.1 us
    all_gather x1, blocking collectives, shards(): lax.all_gather(b_imag, 'fsdp', axis=0, tiled=True)  32.2 us
    all_gather x1, blocking collectives, shards(): lax.all_gather(c_imag, 'fsdp', axis=0, tiled=True)  31 us
    all_gather x1, blocking collectives, shards(): lax.all_gather(w_value, 'fsdp', axis=0, tiled=True)  30.7 us
  transfers between devices with their start and end apart: 15, of which 10 were waited for; matrix products, arithmetic and copies ran while one was open for 8% of the time, Pallas kernels for 0%

profile of v1, /device:TPU:0, one launch (start us, length us, event | category | flops | bytes accessed | tf_op | source)
XLA Modules:
  0.0 1023.4 jit_solution(1246289665687001657)
XLA Ops:
  16.7 23.9 %all-reduce.52 = (bf16[512]{0:T(512)(128)(2,1)}, bf16[512]{0:T(512)(128)(2,1)}, bf16[256]{0:T(256)(128)(2,1)S(1)}, bf16[256]{0:T(256)(128)(2,1)S(1)}, bf16[512]{...) all-reduce(bf16[512]{0:T(512)(128)(2,1)S(1)} %dynamic-update-slice., ...), channel_id=1, replica_groups=mesh['fsdp'=8,'tensor'=4] {'fsdp'}, use_global_device_ids=true, to_apply=%add.40 | all-reduce | flops 3328 | bytes 13312
  42.1 1.7 fusion.16
  46.7 4.0 all-to-all-start
  53.0 31.0 %all_gather.56 = bf16[512,64]{1,0:T(8,128)(2,1)S(1)} all-gather(bf16[64,64]{1,0:T(8,128)(2,1)S(1)} %copy-done.231), channel_id=1, replica_groups=mesh['fsdp'=8,'tensor'=4] {'fsdp'}, dimensions={0}, use_global_device_ids=true | all-gather | bytes 73728 | tf_op jit(solution)/shard_map/all_gather | solution.py:138
  84.0 32.2 %all_gather.53 = bf16[512,64]{1,0:T(8,128)(2,1)} all-gather(bf16[64,64]{1,0:T(8,128)(2,1)S(1)} %copy-done.232), channel_id=1, replica_groups=mesh['fsdp'=8,'tensor'=4] {'fsdp'}, dimensions={0}, use_global_device_ids=true | all-gather | bytes 73728 | tf_op jit(solution)/shard_map/all_gather | solution.py:136
  116.3 30.6 %all_gather.55 = bf16[512,64]{1,0:T(8,128)(2,1)S(1)} all-gather(bf16[64,64]{1,0:T(8,128)(2,1)S(1)} %copy-done.233), channel_id=1, replica_groups=mesh['fsdp'=8,'tensor'=4] {'fsdp'}, dimensions={0}, use_global_device_ids=true | all-gather | bytes 73728 | tf_op jit(solution)/shard_map/all_gather | solution.py:137
  147.7 2.3 broadcast_multiply_fusion
  163.9 5.0 multiply_multiply_fusion.3
  168.9 2.5 fusion.98
  187.6 2.5 copy.194
  190.2 6.0 stack.165
  196.2 1.7 multiply_subtract_fusion.2
  198.6 4.7 fusion.39
  203.9 72.1 %reduce-scatter.18.cloned.1.call-done = f32[1024,512]{1,0:T(8,128)} async-done(((f32[4096,512]{1,0:T(8,128)}), f32[1024,512]{1,0:T(8,128)}) %reduce-scatter.18.cloned.1.call-update) | async-done | bytes 2097168 | tf_op jit(solution)/shard_map/reduce_scatter | solution.py:182
  276.0 3.5 multiply_convert_fusion.1
  279.6 2.6 copy_bitcast_fusion
  282.2 4.3 all-to-all-start.2
  286.6 30.7 %all_gather.59 = bf16[512,128]{1,0:T(8,128)(2,1)S(1)} all-gather(bf16[64,128]{1,0:T(8,128)(2,1)S(1)} %copy-done.234), channel_id=1, replica_groups=mesh['fsdp'=8,'tensor'=4] {'fsdp'}, dimensions={0}, use_global_device_ids=true | all-gather | bytes 147456 | tf_op jit(solution)/shard_map/all_gather | solution.py:139
  317.3 30.5 %all_gather.61 = bf16[512,128]{1,0:T(8,128)(2,1)S(1)} all-gather(bf16[64,128]{1,0:T(8,128)(2,1)S(1)} %copy-done.235), channel_id=1, replica_groups=mesh['fsdp'=8,'tensor'=4] {'fsdp'}, dimensions={0}, use_global_device_ids=true | all-gather | bytes 147456 | tf_op jit(solution)/shard_map/all_gather | solution.py:140
  347.8 4.8 convolution_add_fusion.2
  352.6 6.0 convert_reduce_fusion.1
  360.0 4.6 convolution_add_fusion
  364.7 73.0 %reduce-scatter.20.cloned.1.call-done = f32[1024,512]{1,0:T(8,128)} async-done(((f32[4096,512]{1,0:T(8,128)}), f32[1024,512]{1,0:T(8,128)}) %reduce-scatter.20.cloned.1.call-update) | async-done | bytes 2097168 | tf_op jit(solution)/shard_map/reduce_scatter | solution.py:220
  437.7 4.5 fusion.28
  442.7 2.5 fusion.97
  457.3 19.5 %all-gather.8.cloned.1.call-done = bf16[4096,512]{1,0:T(8,128)(2,1)} async-done(((bf16[1024,512]{1,0:T(8,128)(2,1)}), bf16[4096,512]{1,0:T(8,128)(2,1)}) %all-gather.8.cloned.1.call-update) | async-done | bytes 4194320 | tf_op jit(solution)/shard_map/all_gather | solution.py:229
  476.9 3.6 fusion.71
  480.5 2.4 fusion.96
  493.2 1.5 slice.2051
  494.7 1.5 slice.1933
  497.1 1.5 fusion.102
  498.7 1.5 slice.1925
  500.8 1.6 fusion.100
  506.9 1.5 slice.1928
  508.4 1.6 multiply_subtract_fusion.64
  511.4 1.5 slice.1934
  515.7 1.6 multiply_subtract_fusion.70
  529.5 1.5 slice.1922
  547.4 1.6 slice_add_fusion.17
  549.0 1.7 slice.2054
  558.0 2.5 copy.229
  560.5 7.8 stack.183
  568.3 3.0 multiply_subtract_fusion.1
  571.8 1.9 multiply_reduce_fusion
  575.1 3.0 convolution_convert_fusion
  579.5 4.5 fusion.108
  584.0 1.5 slice_multiply_fusion
  585.5 4.4 all-to-all-start.1
  590.9 4.5 fusion.109
  595.5 3.7 fusion.37
  600.1 6.8 multiply_subtract_fusion
  608.0 3.8 fusion.90
  613.8 2.9 fusion.30
  618.0 10.2 reduce-scatter.22.cloned.1.call-done
  628.2 2.9 fusion.15
  631.1 37.1 %all-reduce.50 = (f32[512]{0:T(512)S(1)}, f32[512]{0:T(512)S(1)}, f32[256]{0:T(256)S(1)}, f32[256]{0:T(256)S(1)}, f32[256]{0:T(256)S(1)}, /*index=5*/f32[512]{0:T(512)S(1)}, f32[512]{0:T(512)S(1)}, f32[512]{0:T(512)S(1)}) all-reduce(f32[512]{0:T(512)S(1)} %get-tuple-element.64, ...), channel_id=5, replica_groups=mesh['fsdp'=8,'tensor'=4] {'fsdp'}, use_global_device_ids=true, to_apply=%region_8.9.clone | all-reduce | flops 3328 | bytes 26624
  668.9 6.3 all-reduce.51
  675.1 3.8 convert_add_fusion.1
  679.0 14.8 %reduce-scatter.24.cloned.1.call-done = f32[64,128]{1,0:T(8,128)} async-done(((f32[512,128]{1,0:T(8,128)}), f32[64,128]{1,0:T(8,128)}) %reduce-scatter.24.cloned.1.call-update) | async-done | bytes 32784 | tf_op jit(solution)/shard_map/reduce_scatter | solution.py:281
  693.7 64.6 %reduce-scatter.26.cloned.1.call-done = f32[64,128]{1,0:T(8,128)} async-done(((f32[512,128]{1,0:T(8,128)}), f32[64,128]{1,0:T(8,128)}) %reduce-scatter.26.cloned.1.call-update) | async-done | bytes 32784 | tf_op jit(solution)/shard_map/reduce_scatter | solution.py:282
  758.3 64.6 %reduce-scatter.34.cloned.1.call-done = f32[64,64]{1,0:T(8,128)} async-done(((f32[512,64]{1,0:T(8,128)}), f32[64,64]{1,0:T(8,128)}) %reduce-scatter.34.cloned.1.call-update) | async-done | bytes 16400
  822.9 64.4 %reduce-scatter.32.cloned.1.call-done = f32[64,64]{1,0:T(8,128)} async-done(((f32[512,64]{1,0:T(8,128)}), f32[64,64]{1,0:T(8,128)}) %reduce-scatter.32.cloned.1.call-update) | async-done | bytes 16400
  887.3 64.6 %reduce-scatter.30.cloned.1.call-done = f32[64,64]{1,0:T(8,128)} async-done(((f32[512,64]{1,0:T(8,128)}), f32[64,64]{1,0:T(8,128)}) %reduce-scatter.30.cloned.1.call-update) | async-done | bytes 16400
  951.9 64.4 %reduce-scatter.28.cloned.1.call-done = f32[64,64]{1,0:T(8,128)} async-done(((f32[512,64]{1,0:T(8,128)}), f32[64,64]{1,0:T(8,128)}) %reduce-scatter.28.cloned.1.call-update) | async-done | bytes 16400
  (975 shorter events, 122.8 us)
Async XLA Ops:
  7.2 37.3 %copy-start = (bf16[1024,512]{1,0:T(8,128)(2,1)S(1)}, bf16[1024,512]{1,0:T(8,128)(2,1)}, u32[]{:S(2)}) copy-start(bf16[1024,512]{1,0:T(8,128)(2,1)} %param.17) | copy-start | bytes 3145732
  7.2 156.7 %all-gather.4.cloned.1.call-start = ((), (), s32[]{:S(2)}) async-start(), calls=%async_computation.12 | async-start | bytes 5242880 | tf_op jit(solution)/shard_map/all_gather | solution.py:163
  42.1 8.7 copy-start.222
  44.4 8.6 copy-start.231
  44.4 39.6 %copy-start.232 = (bf16[64,64]{1,0:T(8,128)(2,1)S(1)}, bf16[64,64]{1,0:T(8,128)(2,1)}, u32[]{:S(2)}) copy-start(bf16[64,64]{1,0:T(8,128)(2,1)} %param.22) | copy-start | bytes 24580
  44.5 71.8 %copy-start.233 = (bf16[64,64]{1,0:T(8,128)(2,1)S(1)}, bf16[64,64]{1,0:T(8,128)(2,1)}, u32[]{:S(2)}) copy-start(bf16[64,64]{1,0:T(8,128)(2,1)} %param.23) | copy-start | bytes 24580
  44.5 103.2 %copy-start.250 = (f32[128]{0:T(128)S(1)}, f32[128]{0:T(128)}, u32[]{:S(2)}) copy-start(f32[128]{0:T(128)} %constant.70.clone.1) | copy-start | bytes 1540
  46.7 116.2 %all-to-all-start = ((bf16[8,2,2048]{2,1,0:T(2,128)(2,1)}), bf16[8,2,2048]{2,1,0:T(2,128)(2,1)}, u32[]{:S(2)}, u32[]{:S(2)}) async-start(bf16[8,2,2048]{2,1,0:T(2,128)(2,1)} %reshape.259), calls=%async_computation | async-start | bytes 131072 | tf_op jit(solution)/shard_map/all_to_all | solution.py:13
  50.7 225.3 %reduce-scatter.18.cloned.1.call-start = ((), (), s32[]{:S(2)}) async-start(), calls=%async_computation.13 | async-start | bytes 10485760 | tf_op jit(solution)/shard_map/reduce_scatter | solution.py:182
  52.2 97.8 %copy-start.246 = (f32[256]{0:T(256)}, f32[256]{0:T(256)S(1)}, u32[]{:S(2)}) copy-start(f32[256]{0:T(256)S(1)} %convert_element_type.102) | copy-start | bytes 3076
  52.2 97.8 %copy-start.248 = (f32[256]{0:T(256)}, f32[256]{0:T(256)S(1)}, u32[]{:S(2)}) copy-start(f32[256]{0:T(256)S(1)} %convert_element_type.97) | copy-start | bytes 3076
  52.3 97.8 %copy-start.252 = (f32[256]{0:T(256)}, f32[256]{0:T(256)S(1)}, u32[]{:S(2)}) copy-start(f32[256]{0:T(256)S(1)} %convert_element_type.98) | copy-start | bytes 3076
  84.0 114.6 %copy-start.36 = (bf16[512,64]{1,0:T(8,128)(2,1)}, bf16[512,64]{1,0:T(8,128)(2,1)S(1)}, u32[]{:S(2)}) copy-start(bf16[512,64]{1,0:T(8,128)(2,1)S(1)} %neg.22) | copy-start | bytes 196612
  146.8 51.8 %copy-start.37 = (bf16[512,64]{1,0:T(8,128)(2,1)}, bf16[512,64]{1,0:T(8,128)(2,1)S(1)}, u32[]{:S(2)}) copy-start(bf16[512,64]{1,0:T(8,128)(2,1)S(1)} %all_gather.55) | copy-start | bytes 196612
  152.3 9.8 copy-start.38
  180.6 5.8 copy-start.90
  180.6 5.8 copy-start.166
  180.7 5.8 copy-start.168
  203.2 72.8 %copy-start.213 = (f32[1024]{0:T(1024)S(1)}, f32[1024]{0:T(1024)}, u32[]{:S(2)}) copy-start(f32[1024]{0:T(1024)} %copy-done.212) | copy-start | bytes 12292
  203.2 72.8 %copy-start.216 = (f32[1024]{0:T(1024)S(1)}, f32[1024]{0:T(1024)}, u32[]{:S(2)}) copy-start(f32[1024]{0:T(1024)} %copy-done.215) | copy-start | bytes 12292
  203.2 72.8 %copy-start.220 = (f32[512]{0:T(512)S(1)}, f32[512]{0:T(512)}, u32[]{:S(2)}) copy-start(f32[512]{0:T(512)} %copy-done.219) | copy-start | bytes 6148
  203.2 72.8 %copy-start.226 = (f32[512]{0:T(512)S(1)}, f32[512]{0:T(512)}, u32[]{:S(2)}) copy-start(f32[512]{0:T(512)} %copy-done.225) | copy-start | bytes 6148
  203.3 144.5 %all-gather.6.cloned.1.call-start = ((), (), s32[]{:S(2)}) async-start(), calls=%async_computation.14 | async-start | bytes 5242880 | tf_op jit(solution)/shard_map/all_gather | solution.py:190
  203.9 233.8 %copy-start.223 = (f32[512]{0:T(512)}, f32[512]{0:T(512)S(1)}, u32[]{:S(2)}) copy-start(f32[512]{0:T(512)S(1)} %convert_element_type.104) | copy-start | bytes 6148
  279.6 6.9 copy-start.256
  279.6 7.0 copy-start.255
  279.6 7.1 copy-start.234
  279.6 37.7 %copy-start.235 = (bf16[64,128]{1,0:T(8,128)(2,1)S(1)}, bf16[64,128]{1,0:T(8,128)(2,1)}, u32[]{:S(2)}) copy-start(bf16[64,128]{1,0:T(8,128)(2,1)} %param.30) | copy-start | bytes 49156
  282.2 70.5 %all-to-all-start.2 = ((bf16[1024,4,128]{2,0,1:T(8,128)(2,1)}), bf16[1024,4,128]{2,0,1:T(8,128)(2,1)}, u32[]{:S(2)}, u32[]{:S(2)}) async-start(bf16[1024,4,128]{2,0,1:T(8,128)(2,1)} %copy_bitcast_fusion), calls=%async_computation.3 | async-start | bytes 2097152 | tf_op jit(solution)/shard_map/all_to_all | solution.py:203
  286.4 151.3 %reduce-scatter.20.cloned.1.call-start = ((), (), s32[]{:S(2)}) async-start(), calls=%async_computation.15 | async-start | bytes 10485760 | tf_op jit(solution)/shard_map/reduce_scatter | solution.py:220
  364.6 112.3 %all-gather.8.cloned.1.call-start = ((), (), s32[]{:S(2)}) async-start(), calls=%async_computation.16 | async-start | bytes 5242880 | tf_op jit(solution)/shard_map/all_gather | solution.py:229
  442.2 186.0 %reduce-scatter.22.cloned.1.call-start = ((), (), s32[]{:S(2)}) async-start(), calls=%async_computation.17 | async-start | bytes 5242880 | tf_op jit(solution)/shard_map/reduce_scatter | solution.py:249
  446.7 9.9 copy-start.40
  446.7 9.9 copy-start.42
  488.9 21.9 %copy-start.103 = (f32[256,64]{1,0:T(8,128)}, f32[256,64]{1,0:T(8,128)S(1)}, u32[]{:S(2)}) copy-start(f32[256,64]{1,0:T(8,128)S(1)} %get-tuple-element.248) | copy-start | bytes 196612
  500.8 28.1 %copy-start.206 = (f32[127,128]{1,0:T(8,128)S(1)}, f32[127,128]{1,0:T(8,128)}, u32[]{:S(2)}) copy-start(f32[127,128]{1,0:T(8,128)} %slice.1920) | copy-start | bytes 195076
  511.4 20.2 %copy-start.211 = (f32[127,128]{1,0:T(8,128)S(1)}, f32[127,128]{1,0:T(8,128)}, u32[]{:S(2)}) copy-start(f32[127,128]{1,0:T(8,128)} %slice.2051) | copy-start | bytes 195076
  547.4 9.2 copy-start.66
  549.0 7.7 copy-start.64
  550.7 5.7 copy-start.156
  550.7 5.8 copy-start.141
  550.7 5.8 copy-start.143
  550.7 6.0 copy-start.137
  550.7 6.0 copy-start.139
  560.5 7.8 copy-start.209
  560.5 7.8 copy-start.210
  578.1 115.6 %reduce-scatter.24.cloned.1.call-start = ((), (), s32[]{:S(2)}) async-start(), calls=%async_computation.18 | async-start | bytes 294912 | tf_op jit(solution)/shard_map/reduce_scatter | solution.py:281
  585.5 89.7 %all-to-all-start.1 = ((bf16[4,1024,128]{2,1,0:T(8,128)(2,1)}), bf16[4,1024,128]{2,1,0:T(8,128)(2,1)}, u32[]{:S(2)}, u32[]{:S(2)}) async-start(bf16[4,1024,128]{2,1,0:T(8,128)(2,1)} %bitcast.523), calls=%async_computation.2 | async-start | bytes 2097152 | tf_op jit(solution)/shard_map/all_to_all | solution.py:199
  589.9 168.4 %reduce-scatter.26.cloned.1.call-start = ((), (), s32[]{:S(2)}) async-start(), calls=%async_computation.19 | async-start | bytes 294912 | tf_op jit(solution)/shard_map/reduce_scatter | solution.py:282
  595.4 227.5 %reduce-scatter.34.cloned.1.call-start = ((), (), s32[]{:S(2)}) async-start(), calls=%async_computation.23 | async-start | bytes 294912
  600.1 8.0 copy-start.2
  600.1 287.3 %reduce-scatter.32.cloned.1.call-start = ((), (), s32[]{:S(2)}) async-start(), calls=%async_computation.22 | async-start | bytes 294912
  607.8 344.2 %reduce-scatter.30.cloned.1.call-start = ((), (), s32[]{:S(2)}) async-start(), calls=%async_computation.21 | async-start | bytes 294912
  613.6 402.8 %reduce-scatter.28.cloned.1.call-start = ((), (), s32[]{:S(2)}) async-start(), calls=%async_computation.20 | async-start | bytes 294912
  613.7 14.5 %copy-start.3 = (bf16[1024,512]{1,0:T(8,128)(2,1)S(1)}, bf16[1024,512]{1,0:T(8,128)(2,1)}, u32[]{:S(2)}) copy-start(bf16[1024,512]{1,0:T(8,128)(2,1)} %fusion.28) | copy-start | bytes 3145732
  613.7 14.5 %copy-start.214 = (f32[1024]{0:T(1024)S(1)}, f32[1024]{0:T(1024)}, u32[]{:S(2)}) copy-start(f32[1024]{0:T(1024)} %copy-done.212) | copy-start | bytes 12292
  613.7 14.5 %copy-start.217 = (f32[1024]{0:T(1024)S(1)}, f32[1024]{0:T(1024)}, u32[]{:S(2)}) copy-start(f32[1024]{0:T(1024)} %copy-done.215) | copy-start | bytes 12292
  613.7 14.5 %copy-start.221 = (f32[512]{0:T(512)S(1)}, f32[512]{0:T(512)}, u32[]{:S(2)}) copy-start(f32[512]{0:T(512)} %copy-done.219) | copy-start | bytes 6148
  613.7 14.5 %copy-start.224 = (f32[512]{0:T(512)S(1)}, f32[512]{0:T(512)}, u32[]{:S(2)}) copy-start(f32[512]{0:T(512)} %copy-done.223) | copy-start | bytes 6148
  613.7 14.5 %copy-start.227 = (f32[512]{0:T(512)S(1)}, f32[512]{0:T(512)}, u32[]{:S(2)}) copy-start(f32[512]{0:T(512)} %copy-done.225) | copy-start | bytes 6148
  616.6 14.5 %copy-start.242 = (f32[512]{0:T(512)S(1)}, f32[512]{0:T(512)}, u32[]{:S(2)}) copy-start(f32[512]{0:T(512)} %copy-done.241) | copy-start | bytes 6148
  616.6 14.5 %copy-start.244 = (f32[512]{0:T(512)S(1)}, f32[512]{0:T(512)}, u32[]{:S(2)}) copy-start(f32[512]{0:T(512)} %copy-done.243) | copy-start | bytes 6148
  616.7 58.5 %copy-start.8 = (bf16[1024,512]{1,0:T(8,128)(2,1)S(1)}, bf16[1024,512]{1,0:T(8,128)(2,1)}, u32[]{:S(2)}) copy-start(bf16[1024,512]{1,0:T(8,128)(2,1)} %param.33) | copy-start | bytes 3145732
  616.7 58.5 %copy-start.229 = (f32[1024]{0:T(1024)S(1)}, f32[1024]{0:T(1024)}, u32[]{:S(2)}) copy-start(f32[1024]{0:T(1024)} %copy-done.228) | copy-start | bytes 12292
  (210 other events, 472.0 us)
Sparse Core Ops, SparseCore 0:
  46.0 31.7 all-gather.3
  203.4 72.5 reduce-scatter.17
  279.6 45.2 all-gather.5
  364.7 72.9 reduce-scatter.19
  442.3 34.4 all-gather.7
  578.2 49.9 reduce-scatter.21
  632.5 61.2 reduce-scatter.23
  698.0 60.3 reduce-scatter.25
  762.6 60.2 reduce-scatter.33
  827.0 60.2 reduce-scatter.31
  891.6 60.2 reduce-scatter.29
  956.0 60.2 reduce-scatter.27
